TPU v7x, 256 devices: a whole 4x4x8 slice. The times are simulated.
256 devices in a mesh: ctx: 16 (over z, core), exp: 16 (over x, y).
Axes of the slice: x: 4, y: 4, z: 8, core: 2. Of those that a mesh axis runs over, the one named last changes fastest.
Arguments:
- inner_input: bfloat16 [8192, 8192], P('ctx', 'exp'), may hold values from -6 to 6
- gate_input: bfloat16 [8192, 8192], P('ctx', 'exp'), may hold values from -6 to 6
- coupling_input: bfloat16 [8192, 256], P('ctx'), may hold values from -6 to 6
- step_input: float32 [8192, 128], P('ctx', 'exp'), may hold values from -7 to 140
- conv_inner: float32 [4, 8192], P(None, 'exp'), may hold values from -3 to 3
- conv_coupling: float32 [4, 256], replicated, may hold values from -3 to 3
- decay_log: float32 [128], P('exp'), may hold values from -5.3 to -2.5
- skip_gain: float32 [128], P('exp'), may hold values from 0.5 to 2
- norm_gain: float32 [8192], P('exp'), may hold values from 0.1 to 1.9
- out_weight: bfloat16 [8192, 4096], P('exp'), may hold values from -0.0625 to 0.0625
- residual: bfloat16 [8192, 4096], P(('ctx', 'exp')), may hold values from -6 to 6
- moe_gain: float32 [4096], replicated, may hold values from 0.1 to 1.9
- router_weight: bfloat16 [4096, 72], replicated, may hold values from -0.1875 to 0.1875
- routes: int32 [8192, 10], P(('ctx', 'exp')), may hold values from 0 to 71, all different within a row
- priority: int32 [256, 32], P(('ctx', 'exp')), may hold values from 0 to 31, each once within a row
- expert_in: bfloat16 [16, 4096, 1536], P('exp', 'ctx'), may hold values from -0.09375 to 0.09375
- expert_out: bfloat16 [16, 4096, 768], P('exp', 'ctx'), may hold values from -0.21875 to 0.21875
Outputs:
- hidden: float32 [8192, 4096], P(('ctx', 'exp'))
- moe_out: float32 [8192, 4096], P(('ctx', 'exp'))
Inputs may be any that keep to these rules, and one draw needn't show every extreme that they name: `routes`: each token names 10 different experts. `priority`: the 32 tokens of each row carry distinct priorities.
All inputs are finite; a program needn't handle non-finite values.
Results may differ from a plain program's by a relative error of at most 0.029.
Values may be sent and summed in bfloat16 or wider, within the bound.
A program may use at most 128 MiB of HBM per device.

v0:
```python
import jax
import jax.numpy as jnp
from jax import lax
from jax.sharding import PartitionSpec as P

HDIM = 64
STATE = 128
KCONV = 4
NEXP = 72
TOPK = 10
FFE = 768
SPAN = 256
INNER = 8192
EPS = 1e-05
HIGH = lax.Precision.HIGHEST


def shifted(array, axis, by):
    devices = lax.axis_size(axis)
    pairs = [(i, i + by) for i in range(devices) if 0 <= i + by < devices]
    return lax.ppermute(array, axis, pairs)


def carried_in(part, axis, combine, identity):
    place = lax.axis_index(axis)
    gathered = jax.tree.map(lambda a: lax.all_gather(a, axis), part)
    state = jax.tree.map(lambda a, e: jnp.zeros_like(a) + jnp.asarray(e, a.dtype), part, identity)

    def one(step, state):
        return combine(
            state, jax.tree.map(lambda a: lax.dynamic_index_in_dim(a, step, 0, False), gathered)
        )

    return lax.fori_loop(0, place, one, state)


def causal_conv(values, before, weight):
    count = values.shape[0]
    padded = jnp.concatenate([before.astype(jnp.float32), values.astype(jnp.float32)], axis=0)
    total = jnp.zeros((count, values.shape[1]), jnp.float32)
    for k in range(KCONV):
        total = total + weight[k][None, :] * padded[k : k + count]
    return jax.nn.silu(total).astype(jnp.bfloat16)


def join_states(earlier, later):
    return (earlier[0] * later[0], later[0][:, None, None] * earlier[1] + later[1])


def body(
    inner_input,
    gate_input,
    coupling_input,
    step_input,
    conv_inner,
    conv_coupling,
    decay_log,
    skip_gain,
    norm_gain,
    out_weight,
    residual,
    moe_gain,
    router_weight,
    routes,
    priority,
    expert_in,
    expert_out,
):
    width = inner_input.shape[1]
    heads = decay_log.shape[0]
    count = inner_input.shape[0]
    blocks = count // SPAN
    edges = jnp.concatenate(
        [inner_input[count - (KCONV - 1) :], coupling_input[count - (KCONV - 1) :]], axis=1
    )
    before = shifted(edges, "ctx", 1)
    inner = causal_conv(inner_input, before[:, :width], conv_inner)
    coupling = causal_conv(coupling_input, before[:, width:], conv_coupling)
    steps = jax.nn.softplus(step_input).reshape(blocks, SPAN, heads)
    inner_parts = inner.reshape(blocks, SPAN, heads, HDIM)
    input_parts = coupling[:, :STATE].reshape(blocks, SPAN, STATE)
    output_parts = coupling[:, STATE:].reshape(blocks, SPAN, STATE)
    rate = steps * (-jnp.exp(decay_log))[None, None, :]
    cums = jnp.cumsum(rate, axis=1)
    scores = jnp.einsum(
        "cin,cjn->cij", output_parts, input_parts, preferred_element_type=jnp.float32
    )
    above = (jnp.arange(SPAN)[:, None] >= jnp.arange(SPAN)[None, :])[None, None]
    flipped = jnp.swapaxes(cums, 1, 2)
    spread = flipped[:, :, :, None] - flipped[:, :, None, :]
    decay = jnp.where(above, jnp.exp(jnp.where(above, spread, 0.0)), 0.0)
    mixing = (scores[:, None] * decay * jnp.swapaxes(steps, 1, 2)[:, :, None, :]).astype(
        jnp.bfloat16
    )
    local = jnp.einsum("chij,cjhp->cihp", mixing, inner_parts, preferred_element_type=jnp.float32)
    inner_wide = inner_parts.astype(jnp.float32)
    tail = jnp.exp(cums[:, -1:, :] - cums) * steps
    states = jnp.einsum(
        "cjh,cjn,cjhp->chnp", tail, input_parts.astype(jnp.float32), inner_wide, precision=HIGH
    )
    drops = jnp.exp(cums[:, -1, :])
    running = jnp.zeros((heads, STATE, HDIM), jnp.float32)
    reach = jnp.ones((heads,), jnp.float32)
    starts = []
    reaches = []
    for k in range(blocks):
        starts.append(running)
        reaches.append(reach)
        running = drops[k][:, None, None] * running + states[k]
        reach = reach * drops[k]
    neutral = (jnp.ones((heads,), jnp.float32), jnp.zeros((heads, STATE, HDIM), jnp.float32))
    incoming = carried_in((reach, running), "ctx", join_states, neutral)[1]
    entry = jnp.stack([reaches[k][:, None, None] * incoming + starts[k] for k in range(blocks)])
    carried = jnp.einsum(
        "cin,cih,chnp->cihp", output_parts.astype(jnp.float32), jnp.exp(cums), entry, precision=HIGH
    )
    mixed = (local + carried + skip_gain[None, None, :, None] * inner_wide).reshape(count, width)
    gated = mixed * jax.nn.silu(gate_input.astype(jnp.float32))
    squares = jnp.sum(gated * gated, axis=1)
    scaled = (gated * norm_gain[None, :]).astype(jnp.bfloat16)
    projected = jnp.dot(scaled, out_weight, preferred_element_type=jnp.float32)
    owned = lax.psum_scatter(
        projected.astype(jnp.bfloat16), "exp", scatter_dimension=0, tiled=True
    ).astype(jnp.float32)
    owned_squares = lax.psum_scatter(squares, "exp", scatter_dimension=0, tiled=True)
    mamba_out = owned * lax.rsqrt(owned_squares / INNER + EPS)[:, None]
    hidden = residual.astype(jnp.float32) + mamba_out
    tokens = hidden.shape[0]
    flight = lax.axis_size("exp")
    capacity = max(2, 2 * tokens * TOPK // NEXP)
    normed = (
        hidden * lax.rsqrt(jnp.mean(hidden * hidden, axis=1) + EPS)[:, None] * moe_gain[None, :]
    ).astype(jnp.bfloat16)
    logits = jnp.dot(normed, router_weight, preferred_element_type=jnp.float32)
    table = routes[:, :, None] == jnp.arange(NEXP, dtype=jnp.int32)[None, None, :]
    picked = jnp.sum(jnp.where(table, logits[:, None, :], 0.0), axis=2)
    raised = jnp.exp(picked)
    probs = raised / jnp.sum(raised, axis=1, keepdims=True)
    match = routes[:, :, None] == jnp.arange(flight, dtype=jnp.int32)[None, None, :]
    member = jnp.sum(match.astype(jnp.int32), axis=1)
    share = jnp.sum(jnp.where(match, probs[:, :, None], 0.0), axis=1).astype(jnp.bfloat16)
    order = priority[0]
    earlier = (order[None, :] < order[:, None]).astype(jnp.int32)
    rank = jnp.sum(earlier[:, :, None] * member[None, :, :], axis=1)
    kept = (member > 0) & (rank < capacity)
    slots = kept[:, :, None] & (
        rank[:, :, None] == jnp.arange(capacity, dtype=jnp.int32)[None, None, :]
    )
    select = jnp.transpose(slots, (1, 2, 0)).astype(jnp.bfloat16)
    outbound = jnp.einsum("fst,td->fsd", select, normed, preferred_element_type=jnp.float32).astype(
        jnp.bfloat16
    )
    arrived = lax.all_to_all(outbound, "exp", split_axis=0, concat_axis=0, tiled=True)
    rows = arrived.reshape(flight * capacity, normed.shape[1])
    slices = lax.axis_size("ctx")
    whole_in = lax.all_gather(expert_in[0], "ctx", axis=0, tiled=True)
    slice_width = rows.shape[1] // slices
    parts = jnp.einsum(
        "rkw,kwf->krf",
        rows.reshape(rows.shape[0], slices, slice_width),
        whole_in.reshape(slices, slice_width, 2 * FFE),
        preferred_element_type=jnp.float32,
    ).astype(jnp.bfloat16)
    units = jnp.sum(lax.optimization_barrier(parts).astype(jnp.float32), axis=0)
    activated = (jax.nn.silu(units[:, :FFE]) * units[:, FFE:]).astype(jnp.bfloat16)
    answer = jnp.einsum(
        "rf,df->rd",
        activated,
        lax.all_gather(expert_out[0], "ctx", axis=0, tiled=True),
        preferred_element_type=jnp.float32,
    ).astype(jnp.bfloat16)
    returned = lax.all_to_all(
        answer.reshape(flight, capacity, answer.shape[1]),
        "exp",
        split_axis=0,
        concat_axis=0,
        tiled=True,
    )
    weights = select * jnp.transpose(share)[:, None, :]
    moe_out = jnp.einsum("fst,fsd->td", weights, returned, preferred_element_type=jnp.float32)
    return (hidden, moe_out)


def solution(mesh):
    placed = (
        P("ctx", "exp"),
        P("ctx", "exp"),
        P("ctx", None),
        P("ctx", "exp"),
        P(None, "exp"),
        P(),
        P("exp"),
        P("exp"),
        P("exp"),
        P("exp", None),
        P(("ctx", "exp"), None),
        P(),
        P(),
        P(("ctx", "exp"), None),
        P(("ctx", "exp"), None),
        P("exp", "ctx", None),
        P("exp", "ctx", None),
    )
    return jax.shard_map(
        body,
        mesh=mesh,
        in_specs=placed,
        out_specs=(P(("ctx", "exp"), None), P(("ctx", "exp"), None)),
        check_vma=False,
    )
```

profile of v0, /device:TPU:32, one launch (start us, length us, event | category | flops | bytes accessed | tf_op | source)
XLA Modules:
  0.0 354.1 jit_solution(14720117451480724429)
XLA Ops:
  8.7 0.8 copy.91
  9.5 1.9 collective-permute-start
  12.9 1.1 reduce-window.6
  15.2 0.8 fusion.66
  16.0 0.9 fusion.65
  17.5 1.0 convert_element_type.80
  18.5 1.3 copy.92
  20.4 1.5 multiply_convert_fusion.9
  22.7 0.8 slice_add_fusion
  23.8 19.0 %all-gather.2 = f32[16,1,8]{2,1,0:T(1,128)} all-gather(f32[1,1,8]{2,1,0:T(1,128)S(1)} %get-tuple-element.98), channel_id=1, replica_groups=mesh['ctx'=16,'exp'=16] {'ctx'}, dimensions={0}, use_global_device_ids=true | all-gather | bytes 544 | tf_op jit(solution)/shard_map/all_gather | solution.py:26
  43.5 1.0 fusion.67
  44.6 24.1 %all-gather.7.cloned.1.call-done = f32[16,8,128,64]{2,3,1,0:T(8,128)} async-done(((f32[1,8,128,64]{2,3,1,0:T(8,128)}), f32[16,8,128,64]{2,3,1,0:T(8,128)}) %all-gather.7.cloned.1.call-update) | async-done | bytes 4194320 | tf_op jit(solution)/shard_map/all_gather | solution.py:26
  68.7 4.1 %while.12 = (s32[]{:T(128)}, f32[8,128,64]{2,1,0:T(8,128)S(1)}, s32[]{:T(128)}, f32[16,8]{1,0:T(8,128)}, f32[16,8,128,64]{2,3,1,0:T(8,128)}, /*index=5*/s32[]{:T(128)}, s32[]{:T(128)}, s32[]{:T(128)}) while((s32[]{:T(128)}, f32[8,128,64]{2,1,0:T(8,128)S(1)}, s32[]{:T(128)}, f32[16,8]{1,0:T(8,128)}, f32[16,8,128,64]{2,3,1,0:T(8,128)}, ...), condition=%wide.region_3.4_spmd, body=%wide.region_2.3_spmd.sunk | while | flops 131077 | bytes 1835231 | solution.py:34
  68.8 1.0 constant_dynamic-slice_fusion.2
  70.8 1.0 constant_dynamic-slice_fusion.2
  73.9 1.5 fusion.68
  75.4 2.3 fusion.17
  77.7 0.8 copy.101
  78.6 1.3 copy-done.10
  79.9 4.6 %convolution_convert_fusion = bf16[512,4096]{1,0:T(8,128)(2,1)} fusion(bf16[512,4096]{1,0:T(8,128)(2,1)S(1)} %copy-done.10, f32[512]{0:T(512)S(1)} %copy-done.11, f32[512,512]{0,1:T(8,128)S(1)} %bitcast.109, bf16[512,512]{0,1:T(8,128)(2,1)S(1)} %copy.102), kind=kOutput, calls=%fused_computation.6 | convolution fusion | flops 2151677952 | bytes 9963520 | tf_op jit(solution)/shard_map/dot_general | solution.py:121
  88.4 40.4 %all-reduce = f32[512]{0:T(512)S(1)} all-reduce(f32[512]{0:T(512)S(1)} %multiply_reduce_fusion), channel_id=5, replica_groups=mesh['ctx'=16,'exp'=16] {'exp'}, use_global_device_ids=true, to_apply=%region_6.7.clone | all-reduce | flops 512 | bytes 4096
  128.9 63.8 %reduce-scatter.2.cloned.1.call-done = bf16[32,4096]{1,0:T(8,128)(2,1)} async-done(((bf16[512,4096]{1,0:T(8,128)(2,1)}), bf16[32,4096]{1,0:T(8,128)(2,1)}) %reduce-scatter.2.cloned.1.call-update) | async-done | bytes 262160 | tf_op jit(solution)/shard_map/reduce_scatter | solution.py:122
  192.6 1.2 multiply_reduce_fusion.1
  194.4 19.8 %all_to_all.10 = bf16[16,8,4096]{2,1,0:T(8,128)(2,1)S(1)} all-to-all(bf16[16,8,4096]{2,1,0:T(8,128)(2,1)S(1)} %convolution_convert_fusion.2), channel_id=1, replica_groups=mesh['ctx'=16,'exp'=16] {'exp'}, dimensions={0} | all-to-all | bytes 2097152 | tf_op jit(solution)/shard_map/all_to_all | solution.py:153
  214.5 53.0 %all-gather.9.cloned.1.call-done = bf16[1,4096,1536]{2,1,0:T(8,128)(2,1)} async-done(((bf16[1,256,1536]{2,1,0:T(8,128)(2,1)}), bf16[1,4096,1536]{2,1,0:T(8,128)(2,1)}) %all-gather.9.cloned.1.call-update) | async-done | bytes 12582928 | tf_op jit(solution)/shard_map/all_gather | solution.py:156
  267.5 6.6 %convolution_convert_fusion.1 = bf16[16,128,1536]{2,1,0:T(8,128)(2,1)S(1)} fusion(bf16[16,256,1536]{2,1,0:T(8,128)(2,1)} %bitcast.107, bf16[128,16,256]{2,1,0:T(8,128)(2,1)S(1)} %bitcast.108), kind=kOutput, calls=%fused_computation.7 | convolution fusion | flops 1613758464 | bytes 19922944 | tf_op jit(solution)/shard_map/rkw,kwf->krf/dot_general | solution.py:158
  274.1 0.9 convert_reduce_fusion
  275.0 40.1 %all-gather.11.cloned.1.call-done = bf16[1,4096,768]{2,1,0:T(8,128)(2,1)} async-done(((bf16[1,256,768]{2,1,0:T(8,128)(2,1)}), bf16[1,4096,768]{2,1,0:T(8,128)(2,1)}) %all-gather.11.cloned.1.call-update) | async-done | bytes 6291472 | tf_op jit(solution)/shard_map/all_gather | solution.py:169
  315.1 5.9 %fusion.5 = bf16[16,8,4096]{2,1,0:T(8,128)(2,1)} fusion(bf16[1,4096,768]{2,1,0:T(8,128)(2,1)} %all-gather.11.cloned.1.call-done, f32[128,1536]{1,0:T(8,128)S(1)} %convert_reduce_fusion), kind=kOutput, calls=%fused_computation.10 | convolution fusion | flops 806420480 | bytes 8126464 | tf_op jit(solution)/shard_map/rf,df->rd/dot_general | solution.py:166
  321.0 6.8 %all-to-all-start.1 = ((bf16[16,8,4096]{2,1,0:T(8,128)(2,1)}), bf16[16,8,4096]{2,1,0:T(8,128)(2,1)S(1)}, u32[]{:S(2)}, u32[]{:S(2)}) async-start(bf16[16,8,4096]{2,1,0:T(8,128)(2,1)} %fusion.5), calls=%async_computation.2 | async-start | bytes 2097152 | tf_op jit(solution)/shard_map/all_to_all | solution.py:172
  328.4 17.6 %all-to-all-done.1 = bf16[16,8,4096]{2,1,0:T(8,128)(2,1)S(1)} async-done(((bf16[16,8,4096]{2,1,0:T(8,128)(2,1)}), bf16[16,8,4096]{2,1,0:T(8,128)(2,1)S(1)}, u32[]{:S(2)}, u32[]{:S(2)}) %all-to-all-start.1) | async-done | bytes 1048608 | tf_op jit(solution)/shard_map/all_to_all | solution.py:172
  346.0 1.5 convolution_bitcast_fusion
  (89 shorter events, 14.8 us)
Async XLA Ops:
  7.2 320.6 %copy-start = (bf16[4096,72]{0,1:T(8,128)(2,1)S(1)}, bf16[4096,72]{0,1:T(8,128)(2,1)}, u32[]{:S(2)}) copy-start(bf16[4096,72]{0,1:T(8,128)(2,1)} %param.31) | copy-start | bytes 1769476
  7.2 61.5 %all-gather.7.cloned.1.call-start = ((), (), s32[]{:S(2)}) async-start(), calls=%async_computation.3 | async-start | bytes 4456448 | tf_op jit(solution)/shard_map/all_gather | solution.py:26
  9.5 10.3 %collective-permute-start = (bf16[3,768]{0,1:T(8,128)(2,1)}, bf16[3,768]{0,1:T(8,128)(2,1)S(1)}, u32[]{:S(2)}, u32[]{:S(2)}) collective-permute-start(bf16[3,768]{0,1:T(8,128)(2,1)} %copy.91), channel_id=1, source_target_pairs={{0,16},{16,32},{32,48},{48,64},{64,80},{80,96},{96,112},{112,128},... | collective-permute-start | bytes 13832 | tf_op jit(solution)/shard_map/ppermute | solution.py:21
  17.5 5.2 %copy-start.8 = (f32[8]{0:T(128)}, f32[8]{0:T(128)S(1)}, u32[]{:S(2)}) copy-start(f32[8]{0:T(128)S(1)} %broadcast_multiply_fusion) | copy-start | bytes 100
  19.7 3.9 %copy-start.4 = (bf16[512,512]{1,0:T(8,128)(2,1)S(1)}, bf16[512,512]{1,0:T(8,128)(2,1)}, u32[]{:S(2)}) copy-start(bf16[512,512]{1,0:T(8,128)(2,1)} %param.20) | copy-start | bytes 1572868
  20.4 48.3 %copy-start.2 = (bf16[512,128]{1,0:T(8,128)(2,1)}, bf16[512,128]{1,0:T(8,128)(2,1)S(1)}, u32[]{:S(2)}) copy-start(bf16[512,128]{1,0:T(8,128)(2,1)S(1)} %get-tuple-element.87) | copy-start | bytes 393220
  23.5 169.1 %reduce-scatter.2.cloned.1.call-start = ((), (), s32[]{:S(2)}) async-start(), calls=%async_computation.4 | async-start | bytes 4456448 | tf_op jit(solution)/shard_map/reduce_scatter | solution.py:122
  72.8 2.5 copy-start.3
  77.7 2.2 copy-start.10
  77.7 2.2 copy-start.11
  84.5 1.4 copy-start.6
  84.5 1.4 copy-start.9
  84.5 2.2 copy-start.12
  84.5 108.1 %copy-start.5 = (bf16[32,4096]{1,0:T(8,128)(2,1)S(1)}, bf16[32,4096]{1,0:T(8,128)(2,1)}, u32[]{:S(2)}) copy-start(bf16[32,4096]{1,0:T(8,128)(2,1)} %param.29) | copy-start | bytes 786436
  84.6 109.3 %copy-start.7 = (f32[4096]{0:T(1024)S(1)}, f32[4096]{0:T(1024)}, u32[]{:S(2)}) copy-start(f32[4096]{0:T(1024)} %param.30) | copy-start | bytes 49156
  84.6 182.9 %all-gather.9.cloned.1.call-start = ((), (), s32[]{:S(2)}) async-start(), calls=%async_computation.5 | async-start | bytes 13369344 | tf_op jit(solution)/shard_map/all_gather | solution.py:156
  85.3 229.7 %all-gather.11.cloned.1.call-start = ((), (), s32[]{:S(2)}) async-start(), calls=%async_computation.6 | async-start | bytes 6684672 | tf_op jit(solution)/shard_map/all_gather | solution.py:169
  193.9 133.9 %copy-start.1 = (f32[32,4096]{1,0:T(8,128)}, f32[32,4096]{1,0:T(8,128)S(1)}, u32[]{:S(2)}) copy-start(f32[32,4096]{1,0:T(8,128)S(1)} %get-tuple-element.83) | copy-start | bytes 1572868
  321.0 25.0 %all-to-all-start.1 = ((bf16[16,8,4096]{2,1,0:T(8,128)(2,1)}), bf16[16,8,4096]{2,1,0:T(8,128)(2,1)S(1)}, u32[]{:S(2)}, u32[]{:S(2)}) async-start(bf16[16,8,4096]{2,1,0:T(8,128)(2,1)} %fusion.5), calls=%async_computation.2 | async-start | bytes 2097152 | tf_op jit(solution)/shard_map/all_to_all | solution.py:172
Sparse Core Ops, SparseCore 0:
  23.6 44.9 all-gather.6
  84.7 107.8 reduce-scatter.1
  194.5 72.9 all-gather.8
  269.2 45.8 all-gather.10
where the time goes:
time: 356 us; the launch traced here: 354 us
  waiting for transfers between devices  200 us (56%)
  blocking collectives  79.3 us (22%)
  matrix products  25.1 us (7%)
  between operations  14.8 us (4%)
  local copies, waits for them, and re-layouts  13.1 us (4%)
  other arithmetic  13.1 us (4%)
  starting transfers between devices  8.84 us (2%)
    reduce_scatter x1, waiting for transfers between devices, body(): lax.psum_scatter(projected.astype(jnp.bfloat16), 'exp', scatter_dimension...  63.8 us
    all_gather x1, waiting for transfers between devices, body(): whole_in = lax.all_gather(expert_in[0], 'ctx', axis=0, tiled=True)  53 us
    unnamed x1, blocking collectives  40.4 us
    all_gather x1, waiting for transfers between devices, body(): lax.all_gather(expert_out[0], 'ctx', axis=0, tiled=True)  40.1 us
    all_gather x1, waiting for transfers between devices, carried_in(): gathered = jax.tree.map(lambda a: lax.all_gather(a, axis), part)  24.1 us
    all_to_all x1, blocking collectives, body(): lax.all_to_all(outbound, 'exp', split_axis=0, concat_axis=0, tiled=True)  19.8 us
    all_gather x1, blocking collectives, carried_in(): gathered = jax.tree.map(lambda a: lax.all_gather(a, axis), part)  19 us
    all_to_all x1, waiting for transfers between devices, body(): lax.all_to_all(answer.reshape(flight, capacity, answer.shape[1]), 'exp',...  17.6 us
  transfers between devices with their start and end apart: 6, of which 5 were waited for; matrix products, arithmetic and copies ran while one was open for 6% of the time, Pallas kernels for 0%

commit v1 on v0

--- a/solution.py
+++ b/solution.py
@@ -153,7 +153,9 @@
     arrived = lax.all_to_all(outbound, "exp", split_axis=0, concat_axis=0, tiled=True)
     rows = arrived.reshape(flight * capacity, normed.shape[1])
     slices = lax.axis_size("ctx")
-    whole_in = lax.all_gather(expert_in[0], "ctx", axis=0, tiled=True)
+    whole_in = jnp.concatenate(
+        lax.all_to_all(jnp.stack([expert_in[0]] * lax.axis_size("ctx")), "ctx", 0, 0), axis=0
+    )
     slice_width = rows.shape[1] // slices
     parts = jnp.einsum(
         "rkw,kwf->krf",

time: 356 us -> 575 us (1.62)
  waiting for transfers between devices: 200 us -> 408 us
  local copies, waits for them, and re-layouts: 13.1 us -> 19.4 us
    all_to_all x0 -> x1, waiting for transfers between devices: none -> 301 us  [body(): lax.all_to_all(jnp.stack([expert_in[0]] * lax.axis_size('ctx')), 'ctx', 0...]
    all_gather x1 -> x0, waiting for transfers between devices: 53 us -> none  [body(): whole_in = lax.all_gather(expert_in[0], 'ctx', axis=0, tiled=True)]
    all_gather x1, waiting for transfers between devices: 40.1 us -> 0.02 us  [body(): lax.all_gather(expert_out[0], 'ctx', axis=0, tiled=True)]
    all_to_all x0 -> x1, starting transfers between devices: none -> 7.51 us  [body(): lax.all_to_all(jnp.stack([expert_in[0]] * lax.axis_size('ctx')), 'ctx', 0...]
  transfers between devices with their start and end apart: 6 -> 6, of which waited for: 5 -> 4; matrix products, arithmetic and copies ran while one was open for 6% -> 4% of each run, Pallas kernels for 0% -> 0%
where the time goes in v1:
time: 575 us; the launch traced here: 573 us
  waiting for transfers between devices  408 us (71%)
  blocking collectives  79.2 us (14%)
  matrix products  24.9 us (4%)
  local copies, waits for them, and re-layouts  19.4 us (3%)
  between operations  14.8 us (3%)
  starting transfers between devices  13.2 us (2%)
  other arithmetic  13.1 us (2%)
    all_to_all x1, waiting for transfers between devices, body(): lax.all_to_all(jnp.stack([expert_in[0]] * lax.axis_size('ctx')), 'ctx', 0...  301 us
    reduce_scatter x1, waiting for transfers between devices, body(): lax.psum_scatter(projected.astype(jnp.bfloat16), 'exp', scatter_dimension...  64.4 us
    unnamed x1, blocking collectives  40.4 us
    all_gather x1, waiting for transfers between devices, carried_in(): gathered = jax.tree.map(lambda a: lax.all_gather(a, axis), part)  24.1 us
    all_to_all x1, blocking collectives, body(): lax.all_to_all(outbound, 'exp', split_axis=0, concat_axis=0, tiled=True)  19.8 us
    all_gather x1, blocking collectives, carried_in(): gathered = jax.tree.map(lambda a: lax.all_gather(a, axis), part)  19 us
    all_to_all x1, waiting for transfers between devices, body(): lax.all_to_all(answer.reshape(flight, capacity, answer.shape[1]), 'exp',...  17.9 us
  transfers between devices with their start and end apart: 6, of which 4 were waited for; matrix products, arithmetic and copies ran while one was open for 4% of the time, Pallas kernels for 0%

profile of v1, /device:TPU:32, one launch (start us, length us, event | category | flops | bytes accessed | tf_op | source)
XLA Modules:
  0.0 572.5 jit_solution(10068644178704366029)
XLA Ops:
  8.7 0.8 copy.91
  9.5 1.9 collective-permute-start
  12.9 1.1 reduce-window.6
  15.2 0.8 fusion.66
  16.0 0.9 fusion.65
  17.5 1.0 convert_element_type.80
  18.5 1.3 copy.92
  20.4 1.5 multiply_convert_fusion.9
  23.8 19.0 %all-gather.1 = f32[16,1,8]{2,1,0:T(1,128)} all-gather(f32[1,1,8]{2,1,0:T(1,128)S(1)} %get-tuple-element.98), channel_id=1, replica_groups=mesh['ctx'=16,'exp'=16] {'ctx'}, dimensions={0}, use_global_device_ids=true | all-gather | bytes 544 | tf_op jit(solution)/shard_map/all_gather | solution.py:26
  43.5 1.0 fusion.67
  44.6 24.1 %all-gather.5.cloned.1.call-done = f32[16,8,128,64]{2,3,1,0:T(8,128)} async-done(((f32[1,8,128,64]{2,3,1,0:T(8,128)}), f32[16,8,128,64]{2,3,1,0:T(8,128)}) %all-gather.5.cloned.1.call-update) | async-done | bytes 4194320 | tf_op jit(solution)/shard_map/all_gather | solution.py:26
  68.7 4.1 while.12
  68.8 1.0 constant_dynamic-slice_fusion.2
  70.8 1.0 constant_dynamic-slice_fusion.2
  73.9 1.5 fusion.68
  75.4 2.3 fusion.17
  77.7 0.8 copy.101
  78.6 1.3 copy-done.11
  79.9 4.5 convolution_convert_fusion
  87.6 40.4 %all-reduce = f32[512]{0:T(512)S(1)} all-reduce(f32[512]{0:T(512)S(1)} %multiply_reduce_fusion), channel_id=4, replica_groups=mesh['ctx'=16,'exp'=16] {'exp'}, use_global_device_ids=true, to_apply=%region_6.7.clone | all-reduce | flops 512 | bytes 4096
  128.1 64.4 %reduce-scatter.2.cloned.1.call-done = bf16[32,4096]{1,0:T(8,128)(2,1)} async-done(((bf16[512,4096]{1,0:T(8,128)(2,1)}), bf16[32,4096]{1,0:T(8,128)(2,1)}) %reduce-scatter.2.cloned.1.call-update) | async-done | bytes 262160 | tf_op jit(solution)/shard_map/reduce_scatter | solution.py:122
  192.5 1.2 multiply_reduce_fusion.1
  194.3 19.8 %all_to_all.15 = bf16[16,8,4096]{2,1,0:T(8,128)(2,1)S(1)} all-to-all(bf16[16,8,4096]{2,1,0:T(8,128)(2,1)S(1)} %convolution_convert_fusion.2), channel_id=1, replica_groups=mesh['ctx'=16,'exp'=16] {'exp'}, dimensions={0} | all-to-all | bytes 2097152 | tf_op jit(solution)/shard_map/all_to_all | solution.py:153
  214.1 5.7 stack.15
  219.7 7.5 %all-to-all-start.1 = ((bf16[16,256,1536]{2,1,0:T(8,128)(2,1)}), bf16[16,256,1536]{2,1,0:T(8,128)(2,1)}, u32[]{:S(2)}, u32[]{:S(2)}) async-start(bf16[16,256,1536]{2,1,0:T(8,128)(2,1)} %stack.15), calls=%async_computation.2 | async-start | bytes 25165824 | tf_op jit(solution)/shard_map/all_to_all | solution.py:157
  228.2 300.5 %all-to-all-done.1 = bf16[16,256,1536]{2,1,0:T(8,128)(2,1)} async-done(((bf16[16,256,1536]{2,1,0:T(8,128)(2,1)}), bf16[16,256,1536]{2,1,0:T(8,128)(2,1)}, u32[]{:S(2)}, u32[]{:S(2)}) %all-to-all-start.1) | async-done | bytes 12582944 | tf_op jit(solution)/shard_map/all_to_all | solution.py:157
  528.8 6.6 %convolution_convert_fusion.1 = bf16[16,128,1536]{2,1,0:T(8,128)(2,1)S(1)} fusion(bf16[16,256,1536]{2,1,0:T(8,128)(2,1)} %all-to-all-done.1, bf16[128,16,256]{2,1,0:T(8,128)(2,1)S(1)} %bitcast.107), kind=kOutput, calls=%fused_computation.7 | convolution fusion | flops 1613758464 | bytes 19922944 | tf_op jit(solution)/shard_map/rkw,kwf->krf/dot_general | solution.py:160
  535.4 0.9 convert_reduce_fusion
  536.3 5.9 %fusion.5 = bf16[16,8,4096]{2,1,0:T(8,128)(2,1)} fusion(bf16[1,4096,768]{2,1,0:T(8,128)(2,1)} %all-gather.7.cloned.1.call-done, f32[128,1536]{1,0:T(8,128)S(1)} %convert_reduce_fusion), kind=kOutput, calls=%fused_computation.10 | convolution fusion | flops 806420480 | bytes 8126464 | tf_op jit(solution)/shard_map/rf,df->rd/dot_general | solution.py:168
  542.2 3.7 all-to-all-start.2
  546.5 17.9 %all-to-all-done.2 = bf16[16,8,4096]{2,1,0:T(8,128)(2,1)S(1)} async-done(((bf16[16,8,4096]{2,1,0:T(8,128)(2,1)}), bf16[16,8,4096]{2,1,0:T(8,128)(2,1)S(1)}, u32[]{:S(2)}, u32[]{:S(2)}) %all-to-all-start.2) | async-done | bytes 1048608 | tf_op jit(solution)/shard_map/all_to_all | solution.py:174
  564.5 1.5 convolution_bitcast_fusion
  (91 shorter events, 15.7 us)
Async XLA Ops:
  7.2 538.8 %copy-start = (bf16[4096,72]{0,1:T(8,128)(2,1)S(1)}, bf16[4096,72]{0,1:T(8,128)(2,1)}, u32[]{:S(2)}) copy-start(bf16[4096,72]{0,1:T(8,128)(2,1)} %param.31) | copy-start | bytes 1769476
  7.2 61.5 %all-gather.5.cloned.1.call-start = ((), (), s32[]{:S(2)}) async-start(), calls=%async_computation.4 | async-start | bytes 4456448 | tf_op jit(solution)/shard_map/all_gather | solution.py:26
  9.5 10.3 %collective-permute-start = (bf16[3,768]{0,1:T(8,128)(2,1)}, bf16[3,768]{0,1:T(8,128)(2,1)S(1)}, u32[]{:S(2)}, u32[]{:S(2)}) collective-permute-start(bf16[3,768]{0,1:T(8,128)(2,1)} %copy.91), channel_id=1, source_target_pairs={{0,16},{16,32},{32,48},{48,64},{64,80},{80,96},{96,112},{112,128},... | collective-permute-start | bytes 13832 | tf_op jit(solution)/shard_map/ppermute | solution.py:21
  17.5 5.2 copy-start.9
  19.7 3.9 copy-start.5
  20.4 48.3 %copy-start.2 = (bf16[512,128]{1,0:T(8,128)(2,1)}, bf16[512,128]{1,0:T(8,128)(2,1)S(1)}, u32[]{:S(2)}) copy-start(bf16[512,128]{1,0:T(8,128)(2,1)S(1)} %get-tuple-element.87) | copy-start | bytes 393220
  23.5 169.0 %reduce-scatter.2.cloned.1.call-start = ((), (), s32[]{:S(2)}) async-start(), calls=%async_computation.5 | async-start | bytes 4456448 | tf_op jit(solution)/shard_map/reduce_scatter | solution.py:122
  72.8 2.5 copy-start.4
  77.7 2.2 copy-start.11
  77.7 2.2 copy-start.12
  84.4 0.7 copy-start.7
  84.4 0.7 copy-start.10
  84.4 1.5 copy-start.13
  84.4 108.1 %copy-start.6 = (bf16[32,4096]{1,0:T(8,128)(2,1)S(1)}, bf16[32,4096]{1,0:T(8,128)(2,1)}, u32[]{:S(2)}) copy-start(bf16[32,4096]{1,0:T(8,128)(2,1)} %param.29) | copy-start | bytes 786436
  84.4 109.3 %copy-start.8 = (f32[4096]{0:T(1024)S(1)}, f32[4096]{0:T(1024)}, u32[]{:S(2)}) copy-start(f32[4096]{0:T(1024)} %param.30) | copy-start | bytes 49156
  84.5 129.6 %copy-start.3 = (bf16[1,256,1536]{2,1,0:T(8,128)(2,1)S(1)}, bf16[1,256,1536]{2,1,0:T(8,128)(2,1)}, u32[]{:S(2)}) copy-start(bf16[1,256,1536]{2,1,0:T(8,128)(2,1)} %param.34) | copy-start | bytes 2359300
  193.7 352.2 %copy-start.1 = (f32[32,4096]{1,0:T(8,128)}, f32[32,4096]{1,0:T(8,128)S(1)}, u32[]{:S(2)}) copy-start(f32[32,4096]{1,0:T(8,128)S(1)} %get-tuple-element.83) | copy-start | bytes 1572868
  219.7 309.0 %all-to-all-start.1 = ((bf16[16,256,1536]{2,1,0:T(8,128)(2,1)}), bf16[16,256,1536]{2,1,0:T(8,128)(2,1)}, u32[]{:S(2)}, u32[]{:S(2)}) async-start(bf16[16,256,1536]{2,1,0:T(8,128)(2,1)} %stack.15), calls=%async_computation.2 | async-start | bytes 25165824 | tf_op jit(solution)/shard_map/all_to_all | solution.py:157
  227.3 309.1 %all-gather.7.cloned.1.call-start = ((), (), s32[]{:S(2)}) async-start(), calls=%async_computation.6 | async-start | bytes 6684672 | tf_op jit(solution)/shard_map/all_gather | solution.py:171
  542.2 22.2 %all-to-all-start.2 = ((bf16[16,8,4096]{2,1,0:T(8,128)(2,1)}), bf16[16,8,4096]{2,1,0:T(8,128)(2,1)S(1)}, u32[]{:S(2)}, u32[]{:S(2)}) async-start(bf16[16,8,4096]{2,1,0:T(8,128)(2,1)} %fusion.5), calls=%async_computation.3 | async-start | bytes 2097152 | tf_op jit(solution)/shard_map/all_to_all | solution.py:174
Sparse Core Ops, SparseCore 0:
  23.6 44.9 all-gather.4
  84.6 107.8 reduce-scatter.1
  229.9 154.7 all-gather.6
